TPU v7x, 128 devices: a whole 4x4x4 slice. The times are simulated.
128 devices in a mesh: req: 32 (over z, x, core), tp: 4 (over y).
Axes of the slice: x: 4, y: 4, z: 4, core: 2. Of those that a mesh axis runs over, the one named last changes fastest.
Arguments:
- tokens: bfloat16 [16384, 2560], P('req'), may hold values from -6 to 6
- lengths: int32 [32], P('req'), may hold values from 1 to 512, as said below
- page_slot: int32 [128], replicated, may hold values from 0 to 127, as said below
- trainer_layout: int32 [128], replicated, may hold values from 0 to 127, each once
- trainer_qkv: float32 [2560, 3840], P(('req', 'tp'))
- trainer_gateup: float32 [2560, 13824], P(('req', 'tp')), may hold values from -0.125 to 0.125
- attn_gain: float32 [2560], replicated, may hold values from 0.1 to 1.9
- ffn_gain: float32 [2560], replicated, may hold values from 0.1 to 1.9
- out_proj: bfloat16 [2560, 2560], P('tp'), may hold values from -0.125 to 0.125
- down_proj: bfloat16 [6912, 2560], P('tp'), may hold values from -0.078125 to 0.078125
Outputs:
- layer_out: bfloat16 [16384, 2560], P(('req', 'tp'))
- kv_cache: bfloat16 [128, 128, 1280], P('req', None, 'tp')
Inputs may be any that keep to these rules, and one draw needn't show every extreme that they name: `lengths`: heavy-tailed; some request has exactly 512. `page_slot`: a permutation; pool slot s belongs to request device s // 4; the 4 pages of one request belong to 4 different devices. `trainer_layout`: a permutation; shard s is the trainer shard on the device with index s over req and tp together.
All inputs are finite; a program needn't handle non-finite values.
Results may differ from a plain program's by a relative error of at most 0.0065.
The roundings to bfloat16 on the way count: a program that leaves them out, or rounds other values in their place, can miss the bound.
Values may be sent and summed in bfloat16 or wider, within the bound.
A program may use at most 192 MiB of HBM per device.

v0:
```python
import jax
import jax.numpy as jnp
from jax import lax
from jax.sharding import PartitionSpec as P

HD = 80
PAGE = 128
eps_norm = 1e-05
theta_base = 10000.0


def normed(values, gain):
    scale = lax.rsqrt(jnp.mean(values * values, axis=-1, keepdims=True) + eps_norm)
    return (values * scale * gain).astype(jnp.bfloat16)


def rotary(field, head_dim):
    half = head_dim // 2
    count = field.shape[0]
    freq = theta_base ** (-jnp.arange(half, dtype=jnp.float32) * 2.0 / head_dim)
    angles = jnp.arange(count, dtype=jnp.float32)[:, None] * freq[None, :]
    cosine = jnp.cos(angles)[:, None, :]
    sine = jnp.sin(angles)[:, None, :]
    first = field[..., :half]
    second = field[..., half:]
    return jnp.concatenate(
        [first * cosine - second * sine, second * cosine + first * sine], axis=-1
    )


def body(
    tokens,
    lengths,
    page_slot,
    trainer_layout,
    trainer_qkv,
    trainer_gateup,
    attn_gain,
    ffn_gain,
    out_proj,
    down_proj,
):
    n_tp = lax.axis_size("tp")
    n_req = lax.axis_size("req")
    devices = n_tp * n_req
    rows_each = trainer_qkv.shape[0]
    seq_len = tokens.shape[0]
    model_dim = tokens.shape[1]
    head_dim = HD
    local_heads = out_proj.shape[0] // head_dim
    group_cols = trainer_qkv.shape[1] // n_tp
    local_kv = (group_cols // head_dim - local_heads) // 2
    group = local_heads // local_kv
    q_cols = local_heads * head_dim
    k_cols = local_kv * head_dim
    ff_local = down_proj.shape[0]
    qkv_half, gu_half = (
        lax.all_to_all(
            trainer_qkv.astype(jnp.bfloat16), "tp", split_axis=1, concat_axis=0, tiled=True
        ),
        lax.all_to_all(
            trainer_gateup.astype(jnp.bfloat16), "tp", split_axis=1, concat_axis=0, tiled=True
        ),
    )
    x_f = tokens.astype(jnp.float32)
    x_norm = normed(x_f, attn_gain)
    row_of = (trainer_layout[:, None] * rows_each + jnp.arange(rows_each, dtype=jnp.int32)).reshape(
        1, -1
    )
    place = (jnp.arange(model_dim, dtype=jnp.int32)[:, None] == row_of).astype(jnp.bfloat16)
    x_norm = jnp.dot(x_norm, place, preferred_element_type=jnp.float32).astype(jnp.bfloat16)
    qkv_weight = lax.all_gather(qkv_half, "req", axis=0, tiled=True)
    gu_weight = lax.all_gather(gu_half, "req", axis=0, tiled=True)
    joined = jnp.dot(x_norm, qkv_weight, preferred_element_type=jnp.float32)
    query = rotary(joined[:, :q_cols].reshape(seq_len, local_heads, head_dim), head_dim)
    keys = rotary(
        joined[:, q_cols : q_cols + k_cols].reshape(seq_len, local_kv, head_dim), head_dim
    )
    query16 = query.astype(jnp.bfloat16).reshape(seq_len, local_kv, group, head_dim)
    keys16 = keys.astype(jnp.bfloat16)
    values16 = (
        joined[:, q_cols + k_cols :].reshape(seq_len, local_kv, head_dim).astype(jnp.bfloat16)
    )
    scores = jnp.einsum(
        "qkgd,skd->kgqs", query16, keys16, preferred_element_type=jnp.float32
    ) * head_dim ** (-0.5)
    slots = jnp.arange(seq_len, dtype=jnp.int32)
    length = lengths[0]
    allowed = (slots[None, :] <= slots[:, None]) & (slots[None, :] < length)
    scores = jnp.where(allowed[None, None], scores, -1e30)
    probs = jax.nn.softmax(scores, axis=-1).astype(jnp.bfloat16)
    context = jnp.einsum(
        "kgqs,skd->qkgd", probs, values16, preferred_element_type=jnp.float32
    ).astype(jnp.bfloat16)
    partial_out = jnp.dot(
        context.reshape(seq_len, q_cols), out_proj, preferred_element_type=jnp.float32
    )
    share = seq_len // n_tp
    tp_index = lax.axis_index("tp")
    mixed = lax.psum_scatter(
        partial_out.astype(jnp.bfloat16), "tp", scatter_dimension=0, tiled=True
    )
    x_share = lax.dynamic_slice_in_dim(tokens, tp_index * share, share, 0)
    resid_share = x_share.astype(jnp.float32) + mixed.astype(jnp.float32)
    h_share = normed(resid_share, ffn_gain)
    h_share = jnp.dot(h_share, place, preferred_element_type=jnp.float32).astype(jnp.bfloat16)
    h_norm = lax.all_gather(h_share, "tp", axis=0, tiled=True)
    projected = jnp.dot(h_norm, gu_weight, preferred_element_type=jnp.float32)
    hidden = (jax.nn.silu(projected[:, :ff_local]) * projected[:, ff_local:]).astype(jnp.bfloat16)
    down = jnp.dot(hidden, down_proj, preferred_element_type=jnp.float32)
    added = lax.psum_scatter(
        down.astype(jnp.bfloat16), "tp", scatter_dimension=0, tiled=True
    ).astype(jnp.float32)
    share_slots = tp_index * share + jnp.arange(share, dtype=jnp.int32)
    live_share = (share_slots < length).astype(jnp.float32)
    layer_out = ((resid_share + added) * live_share[:, None]).astype(jnp.bfloat16)
    live_rows = (slots < length)[:, None]
    key_rows = keys16.reshape(seq_len, k_cols)
    value_rows = values16.reshape(seq_len, k_cols)
    cache_rows = jnp.concatenate(
        [
            jnp.where(live_rows, key_rows, jnp.zeros_like(key_rows)),
            jnp.where(live_rows, value_rows, jnp.zeros_like(value_rows)),
        ],
        axis=1,
    )
    pages = cache_rows.reshape(seq_len // PAGE, PAGE, 2 * k_cols)
    pool_size = pages.shape[0]
    owner = lax.axis_index("req")
    targets = owner * pool_size + jnp.arange(pool_size, dtype=jnp.int32)
    picks = (page_slot[:, None] == targets[None, :]).astype(jnp.bfloat16)
    pool = jnp.einsum(
        "np,nsc->psc",
        picks,
        lax.all_gather(pages, "req", axis=0, tiled=True),
        preferred_element_type=jnp.float32,
    )
    kv_cache = pool.astype(jnp.bfloat16)
    return (layer_out, kv_cache)


def solution(mesh):
    return jax.shard_map(
        body,
        mesh=mesh,
        in_specs=(
            P("req", None),
            P("req"),
            P(),
            P(),
            P(("req", "tp"), None),
            P(("req", "tp"), None),
            P(),
            P(),
            P("tp", None),
            P("tp", None),
        ),
        out_specs=(P(("req", "tp"), None), P("req", None, "tp")),
        check_vma=False,
    )
```

profile of v0, /device:TPU:1, one launch (start us, length us, event | category | flops | bytes accessed | tf_op | source)
XLA Modules:
  0.0 364.6 jit_solution(9727156666313900420)
XLA Ops:
  7.2 1.2 convert_element_type.84
  8.4 0.9 all_to_all.28
  9.3 1.0 copy.18
  10.3 10.0 %all_to_all.38 = bf16[20,4,960]{2,0,1:T(8,128)(2,1)S(1)} all-to-all(bf16[20,4,960]{2,0,1:T(8,128)(2,1)S(1)} %copy.18), channel_id=1, replica_groups=mesh['req'=32,'tp'=4] {'tp'}, dimensions={1} | all-to-all | bytes 307200 | tf_op jit(solution)/shard_map/all_to_all | solution.py:58
  20.3 0.7 all_to_all.31
  21.7 0.7 broadcast_multiply_fusion
  22.6 2.3 fusion.8
  24.9 0.4 fusion.39
  25.3 0.9 fusion.27
  26.2 44.8 %all-gather.5.cloned.1.call-done = bf16[2560,960]{1,0:T(8,128)(2,1)} async-done(((bf16[80,960]{1,0:T(8,128)(2,1)}), bf16[2560,960]{1,0:T(8,128)(2,1)}) %all-gather.5.cloned.1.call-update) | async-done | bytes 4915216 | tf_op jit(solution)/shard_map/all_gather | solution.py:72
  70.9 14.3 %fusion.57 = f32[512,960]{0,1:T(8,128)} fusion(bf16[2560,960]{1,0:T(8,128)(2,1)} %all-gather.5.cloned.1.call-done, s32[2560]{0:T(1024)S(1)} %add.92, bf16[512,2560]{1,0:T(8,128)(2,1)} %param.10, f32[2560]{0:T(1024)S(1)} %copy-done.7, f32[512]{0:T(512)S(1)} %add_rsqrt_fusion), kind=kOutput, calls=%fused_computation.79 | convolution fusion | flops 9240576000 | bytes 9525248 | tf_op jit(solution)/shard_map/dot_general | solution.py:74
  85.2 1.8 select_bitcast_fusion
  87.1 1.0 subtract_convert_fusion
  88.1 0.7 multiply_subtract_fusion
  88.8 7.8 %fusion.52 = (f32[2,4,512]{2,1,0:T(4,128)S(1)}, f32[2,4,512,512]{2,3,1,0:T(8,128)}) fusion(pred[512,512]{0,1:T(8,128)(4,1)} %fusion.27, bf16[512,2,4,40]{0,3,2,1:T(8,128)(2,1)} %bitcast.67, bf16[512,2,4,40]{0,3,2,1:T(8,128)(2,1)} %bitcast.66, bf16[512,2,40]{0,2,1:T(8,128)(2,1)} %get-tuple-element.13, bf16[512,2,40]{0,2,1:T(8,128)(2,1)S(1)} %get-tuple-element.12), kind=kOutput, calls=%fused_computation.78 | convolution fusion | flops 345571840 | bytes 9486336 | tf_op jit(solution)/shard_map/sub | solution.py:91
  96.6 4.2 %fusion.23 = bf16[2,80,4,512]{3,1,2,0:T(8,128)(2,1)S(1)} fusion(bf16[512,2,80,1]{0,2,3,1:T(8,128)(2,1)S(1)} %bitcast.68, f32[2,4,512,512]{2,3,1,0:T(8,128)} %get-tuple-element.17, f32[2,4,512]{2,1,0:T(4,128)S(1)} %get-tuple-element.16), kind=kOutput, calls=%fused_computation.30 | convolution fusion | flops 340066304 | bytes 9224192 | tf_op jit(solution)/shard_map/kgqs,skd->qkgd/dot_general | solution.py:92
  100.8 3.8 %convolution_convert_fusion.1 = bf16[512,2560]{1,0:T(8,128)(2,1)} fusion(bf16[512,640]{0,1:T(8,128)(2,1)S(1)} %bitcast.64, bf16[640,2560]{1,0:T(8,128)(2,1)S(1)} %copy-done), kind=kOutput, calls=%fused_computation.19 | convolution fusion | flops 1679032320 | bytes 6553600 | tf_op jit(solution)/shard_map/dot_general | solution.py:95
  104.7 33.0 %reduce-scatter.3.cloned.1.call-done = bf16[128,2560]{1,0:T(8,128)(2,1)} async-done(((bf16[512,2560]{1,0:T(8,128)(2,1)}), bf16[128,2560]{1,0:T(8,128)(2,1)}) %reduce-scatter.3.cloned.1.call-update) | async-done | bytes 655376 | tf_op jit(solution)/shard_map/reduce_scatter | solution.py:100
  137.7 1.6 multiply_reduce_fusion
  139.3 8.0 %fusion.17 = bf16[128,2560]{1,0:T(8,128)(2,1)} fusion(s32[2560]{0:T(1024)S(1)} %add.92, bf16[128,2560]{1,0:T(8,128)(2,1)} %reduce-scatter.3.cloned.1.call-done, f32[2560]{0:T(1024)S(1)} %copy-done.8, f32[128]{0:T(128)S(1)} %add_rsqrt_fusion.1, bf16[512,2560]{1,0:T(8,128)(2,1)} %param.10, s32[]{:T(128)S(6)} %select_n.15), kind=kOutput, calls=%fused_computation.26 | convolution fusion | flops 1686568960 | bytes 1987076 | tf_op jit(solution)/shard_map/dot_general | solution.py:106
  147.8 12.4 %all_to_all.39 = bf16[20,4,3456]{2,0,1:T(8,128)(2,1)S(1)} all-to-all(bf16[20,4,3456]{2,0,1:T(8,128)(2,1)S(1)} %copy.20), channel_id=1, replica_groups=mesh['req'=32,'tp'=4] {'tp'}, dimensions={1} | all-to-all | bytes 1105920 | tf_op jit(solution)/shard_map/all_to_all | solution.py:61
  160.2 0.9 all_to_all.35
  161.4 0.7 pad_maximum_fusion.7
  162.4 20.4 %all-gather.7.cloned.1.call-done = bf16[512,2560]{1,0:T(8,128)(2,1)} async-done(((bf16[128,2560]{1,0:T(8,128)(2,1)}), bf16[512,2560]{1,0:T(8,128)(2,1)}) %all-gather.7.cloned.1.call-update) | async-done | bytes 2621456 | tf_op jit(solution)/shard_map/all_gather | solution.py:107
  182.9 76.9 %all-gather.9.cloned.1.call-done = bf16[2560,3456]{1,0:T(8,128)(2,1)} async-done(((bf16[80,3456]{1,0:T(8,128)(2,1)}), bf16[2560,3456]{1,0:T(8,128)(2,1)}) %all-gather.9.cloned.1.call-update) | async-done | bytes 17694736 | tf_op jit(solution)/shard_map/all_gather | solution.py:73
  259.8 14.5 %fusion.58 = f32[512,3456]{1,0:T(8,128)S(1)} fusion(bf16[512,2560]{1,0:T(8,128)(2,1)} %all-gather.7.cloned.1.call-done, bf16[2560,3456]{1,0:T(8,128)(2,1)} %all-gather.9.cloned.1.call-done), kind=kOutput, calls=%fused_computation.80 | convolution fusion | flops 9059696640 | bytes 27394048 | tf_op jit(solution)/shard_map/dot_general | solution.py:108
  274.3 10.0 %convolution_convert_fusion = bf16[512,2560]{1,0:T(8,128)(2,1)} fusion(bf16[1728,2560]{1,0:T(8,128)(2,1)} %param.19, f32[512,3456]{1,0:T(8,128)S(1)} %fusion.58), kind=kOutput, calls=%fused_computation.18 | convolution fusion | flops 4536467456 | bytes 18808832 | tf_op jit(solution)/shard_map/dot_general | solution.py:110
  284.4 35.4 %all-gather.11.cloned.1.call-done = bf16[128,128,320]{1,2,0:T(8,128)(2,1)} async-done(((bf16[4,128,320]{1,2,0:T(8,128)(2,1)}), bf16[128,128,320]{1,2,0:T(8,128)(2,1)}) %all-gather.11.cloned.1.call-update) | async-done | bytes 10485776 | tf_op jit(solution)/shard_map/all_gather | solution.py:135
  319.8 9.8 %fusion.24 = bf16[4,128,320]{1,0,2:T(4,128)(2,1)S(1)} fusion(bf16[128,128,320]{1,2,0:T(8,128)(2,1)} %all-gather.11.cloned.1.call-done, s32[128]{0:T(128)S(1)} %copy-done.6, s32[4]{0:T(128)S(1)} %iota_add_fusion.1), kind=kOutput, calls=%fused_computation.35 | convolution fusion | flops 42107392 | bytes 10813968 | tf_op jit(solution)/shard_map/np,nsc->psc/dot_general | solution.py:132
  329.6 0.8 copy.24
  330.3 24.9 %reduce-scatter.5.cloned.1.call-done = bf16[128,2560]{1,0:T(8,128)(2,1)} async-done(((bf16[512,2560]{1,0:T(8,128)(2,1)}), bf16[128,2560]{1,0:T(8,128)(2,1)}) %reduce-scatter.5.cloned.1.call-update) | async-done | bytes 655376 | tf_op jit(solution)/shard_map/reduce_scatter | solution.py:111
  355.2 2.6 multiply_convert_fusion
  (50 shorter events, 1.3 us)
Async XLA Ops:
  7.2 93.7 %copy-start = (bf16[640,2560]{1,0:T(8,128)(2,1)S(1)}, bf16[640,2560]{1,0:T(8,128)(2,1)}, u32[]{:S(2)}) copy-start(bf16[640,2560]{1,0:T(8,128)(2,1)} %param.18) | copy-start | bytes 9830404
  7.2 63.8 %copy-start.7 = (f32[2560]{0:T(1024)S(1)}, f32[2560]{0:T(1024)}, u32[]{:S(2)}) copy-start(f32[2560]{0:T(1024)} %param.16) | copy-start | bytes 30724
  7.2 63.7 %all-gather.5.cloned.1.call-start = ((), (), s32[]{:S(2)}) async-start(), calls=%async_computation.4 | async-start | bytes 5406720 | tf_op jit(solution)/shard_map/all_gather | solution.py:72
  21.0 116.7 %reduce-scatter.3.cloned.1.call-start = ((), (), s32[]{:S(2)}) async-start(), calls=%async_computation.5 | async-start | bytes 3276800 | tf_op jit(solution)/shard_map/reduce_scatter | solution.py:100
  85.2 1.9 slice-start.1
  85.2 2.9 slice-start
  88.8 7.8 %copy-start.5 = (bf16[512,160]{0,1:T(8,128)(2,1)S(1)}, bf16[512,160]{0,1:T(8,128)(2,1)}, u32[]{:S(2)}) copy-start(bf16[512,160]{0,1:T(8,128)(2,1)} %get-tuple-element.9) | copy-start | bytes 491524
  100.8 38.5 %copy-start.8 = (f32[2560]{0:T(1024)S(1)}, f32[2560]{0:T(1024)}, u32[]{:S(2)}) copy-start(f32[2560]{0:T(1024)} %param.17) | copy-start | bytes 30724
  104.6 78.2 %all-gather.7.cloned.1.call-start = ((), (), s32[]{:S(2)}) async-start(), calls=%async_computation.6 | async-start | bytes 3276800 | tf_op jit(solution)/shard_map/all_gather | solution.py:107
  139.3 8.1 %copy-start.2 = (f32[20,13824]{1,0:T(8,128)S(1)}, f32[20,13824]{1,0:T(8,128)}, u32[]{:S(2)}) copy-start(f32[20,13824]{1,0:T(8,128)} %param.15) | copy-start | bytes 3317764
  147.3 13.9 %copy-start.3 = (bf16[20,4,8,128]{3,2,1,0:T(8,128)(2,1)S(1)}, bf16[20,4,8,128]{3,2,1,0:T(8,128)(2,1)}, u32[]{:S(2)}) copy-start(bf16[20,4,8,128]{3,2,1,0:T(8,128)(2,1)} %get-tuple-element.8) | copy-start | bytes 491524
  147.3 14.0 %copy-start.4 = (bf16[512,2,40]{0,2,1:T(8,128)(2,1)S(1)}, bf16[512,2,40]{0,2,1:T(8,128)(2,1)}, u32[]{:S(2)}) copy-start(bf16[512,2,40]{0,2,1:T(8,128)(2,1)} %get-tuple-element.13) | copy-start | bytes 245764
  147.3 112.5 %all-gather.9.cloned.1.call-start = ((), (), s32[]{:S(2)}) async-start(), calls=%async_computation.7 | async-start | bytes 18247680 | tf_op jit(solution)/shard_map/all_gather | solution.py:73
  161.2 158.6 %all-gather.11.cloned.1.call-start = ((), (), s32[]{:S(2)}) async-start(), calls=%async_computation.9 | async-start | bytes 10813440 | tf_op jit(solution)/shard_map/all_gather | solution.py:135
  162.2 193.0 %reduce-scatter.5.cloned.1.call-start = ((), (), s32[]{:S(2)}) async-start(), calls=%async_computation.8 | async-start | bytes 3276800 | tf_op jit(solution)/shard_map/reduce_scatter | solution.py:111
  274.3 45.5 %copy-start.6 = (s32[128]{0:T(128)S(1)}, s32[128]{0:T(128)}, u32[]{:S(2)}) copy-start(s32[128]{0:T(128)} %param.12) | copy-start | bytes 1540
  319.8 38.0 %copy-start.1 = (bf16[640,2560]{1,0:T(8,128)(2,1)S(1)}, bf16[640,2560]{1,0:T(8,128)(2,1)}, u32[]{:S(2)}) copy-start(bf16[640,2560]{1,0:T(8,128)(2,1)} %param.18) | copy-start | bytes 9830404
Sparse Core Ops, SparseCore 0:
  21.2 49.7 all-gather.4
  104.7 32.9 reduce-scatter.2
  147.4 35.3 all-gather.6
  185.0 74.6 all-gather.8
  262.5 57.3 all-gather.10
  322.1 33.0 reduce-scatter.4
where the time goes:
time: 365 us
  waiting for transfers between devices  236 us (65%)
  matrix products  72.3 us (20%)
  blocking collectives  22.4 us (6%)
  between operations  15 us (4%)
  other arithmetic  14.1 us (4%)
  local copies, waits for them, and re-layouts  4.84 us (1%)
    all_gather x1, waiting for transfers between devices, body(): gu_weight = lax.all_gather(gu_half, 'req', axis=0, tiled=True)  76.9 us
    all_gather x1, waiting for transfers between devices, body(): qkv_weight = lax.all_gather(qkv_half, 'req', axis=0, tiled=True)  44.8 us
    all_gather x1, waiting for transfers between devices, body(): lax.all_gather(pages, 'req', axis=0, tiled=True)  35.4 us
    reduce_scatter x1, waiting for transfers between devices, body(): lax.psum_scatter(partial_out.astype(jnp.bfloat16), 'tp', scatter_dimensio...  33 us
    reduce_scatter x1, waiting for transfers between devices, body(): lax.psum_scatter(down.astype(jnp.bfloat16), 'tp', scatter_dimension=0, ti...  24.9 us
    all_gather x1, waiting for transfers between devices, body(): h_norm = lax.all_gather(h_share, 'tp', axis=0, tiled=True)  20.4 us
    dot_general x1, matrix products, body(): projected = jnp.dot(h_norm, gu_weight, preferred_element_type=jnp.float32)  14.5 us
    dot_general x1, matrix products, body(): joined = jnp.dot(x_norm, qkv_weight, preferred_element_type=jnp.float32)  14.3 us
  transfers between devices with their start and end apart: 6, of which 6 were waited for; matrix products, arithmetic and copies ran while one was open for 11% of the time, Pallas kernels for 0%

commit v1 on v0

--- a/solution.py
+++ b/solution.py
@@ -7,6 +7,11 @@
 PAGE = 128
 eps_norm = 1e-05
 theta_base = 10000.0
+
+
+def all_by_exchange(x, axis, dim):
+    sent = jnp.stack([x] * lax.axis_size(axis))
+    return jnp.concatenate(lax.all_to_all(sent, axis, 0, 0), axis=dim)
 
 
 def normed(values, gain):
@@ -69,7 +74,7 @@
     )
     place = (jnp.arange(model_dim, dtype=jnp.int32)[:, None] == row_of).astype(jnp.bfloat16)
     x_norm = jnp.dot(x_norm, place, preferred_element_type=jnp.float32).astype(jnp.bfloat16)
-    qkv_weight = lax.all_gather(qkv_half, "req", axis=0, tiled=True)
+    qkv_weight = all_by_exchange(qkv_half, "req", 0)
     gu_weight = lax.all_gather(gu_half, "req", axis=0, tiled=True)
     joined = jnp.dot(x_norm, qkv_weight, preferred_element_type=jnp.float32)
     query = rotary(joined[:, :q_cols].reshape(seq_len, local_heads, head_dim), head_dim)

time: 365 us -> 391 us (1.071)
  waiting for transfers between devices: 236 us -> 248 us
  starting transfers between devices: 0.47 us -> 10.6 us
  local copies, waits for them, and re-layouts: 4.84 us -> 8.79 us
    all_to_all x0 -> x1, waiting for transfers between devices: none -> 57 us  [all_by_exchange(): return jnp.concatenate(lax.all_to_all(sent, axis, 0, 0), axis=dim)]
    all_gather x1 -> x0, waiting for transfers between devices: 44.8 us -> none  [body(): qkv_weight = lax.all_gather(qkv_half, 'req', axis=0, tiled=True)]
    all_to_all x0 -> x1, starting transfers between devices: none -> 10.2 us  [all_by_exchange(): return jnp.concatenate(lax.all_to_all(sent, axis, 0, 0), axis=dim)]
    another operation x0 -> x2, local copies, waits for them, and re-layouts: none -> 4.66 us  [all_by_exchange(): sent = jnp.stack([x] * lax.axis_size(axis))]
  transfers between devices with their start and end apart: 6 -> 6, of which waited for: 6 -> 6; matrix products, arithmetic and copies ran while one was open for 11% -> 10% of each run, Pallas kernels for 0% -> 0%
where the time goes in v1:
time: 391 us; the launch traced here: 390 us
  waiting for transfers between devices  248 us (63%)
  matrix products  72.3 us (18%)
  blocking collectives  22.4 us (6%)
  between operations  14.7 us (4%)
  other arithmetic  13.4 us (3%)
  starting transfers between devices  10.6 us (3%)
  local copies, waits for them, and re-layouts  8.79 us (2%)
    all_gather x1, waiting for transfers between devices, body(): gu_weight = lax.all_gather(gu_half, 'req', axis=0, tiled=True)  77.1 us
    all_to_all x1, waiting for transfers between devices, all_by_exchange(): return jnp.concatenate(lax.all_to_all(sent, axis, 0, 0), axis=dim)  57 us
    all_gather x1, waiting for transfers between devices, body(): lax.all_gather(pages, 'req', axis=0, tiled=True)  35.4 us
    reduce_scatter x1, waiting for transfers between devices, body(): lax.psum_scatter(partial_out.astype(jnp.bfloat16), 'tp', scatter_dimensio...  32.8 us
    reduce_scatter x1, waiting for transfers between devices, body(): lax.psum_scatter(down.astype(jnp.bfloat16), 'tp', scatter_dimension=0, ti...  24.9 us
    all_gather x1, waiting for transfers between devices, body(): h_norm = lax.all_gather(h_share, 'tp', axis=0, tiled=True)  20.5 us
    dot_general x1, matrix products, body(): projected = jnp.dot(h_norm, gu_weight, preferred_element_type=jnp.float32)  14.5 us
    dot_general x1, matrix products, body(): joined = jnp.dot(x_norm, qkv_weight, preferred_element_type=jnp.float32)  14.3 us
  transfers between devices with their start and end apart: 6, of which 6 were waited for; matrix products, arithmetic and copies ran while one was open for 10% of the time, Pallas kernels for 0%

profile of v1, /device:TPU:1, one launch (start us, length us, event | category | flops | bytes accessed | tf_op | source)
XLA Modules:
  0.0 390.0 jit_solution(16695766590954406069)
XLA Ops:
  7.2 1.2 convert_element_type.84
  8.3 0.9 all_to_all.29
  9.3 1.0 copy.18
  10.2 10.0 %all_to_all.40 = bf16[20,4,960]{2,0,1:T(8,128)(2,1)S(1)} all-to-all(bf16[20,4,960]{2,0,1:T(8,128)(2,1)S(1)} %copy.18), channel_id=1, replica_groups=mesh['req'=32,'tp'=4] {'tp'}, dimensions={1} | all-to-all | bytes 307200 | tf_op jit(solution)/shard_map/all_to_all | solution.py:63
  20.2 0.7 stack.4
  21.0 3.9 %stack.5 = bf16[32,80,960]{2,1,0:T(8,128)(2,1)} broadcast(bf16[80,960]{1,0:T(8,128)(2,1)} %stack.4), dimensions={1,2} | broadcast | bytes 5068800 | tf_op jit(solution)/shard_map/stack | solution.py:13
  24.9 10.2 %all-to-all-start.1 = ((bf16[32,80,960]{2,1,0:T(8,128)(2,1)}), bf16[32,80,960]{2,1,0:T(8,128)(2,1)}, u32[]{:S(2)}, u32[]{:S(2)}) async-start(bf16[32,80,960]{2,1,0:T(8,128)(2,1)} %stack.5), calls=%async_computation.1 | async-start | bytes 10485760 | tf_op jit(solution)/shard_map/all_to_all | solution.py:14
  36.1 2.3 fusion.8
  38.8 0.9 fusion.27
  39.6 57.0 %all-to-all-done.1 = bf16[32,80,960]{2,1,0:T(8,128)(2,1)} async-done(((bf16[32,80,960]{2,1,0:T(8,128)(2,1)}), bf16[32,80,960]{2,1,0:T(8,128)(2,1)}, u32[]{:S(2)}, u32[]{:S(2)}) %all-to-all-start.1) | async-done | bytes 4915232 | tf_op jit(solution)/shard_map/all_to_all | solution.py:14
  96.6 14.3 %fusion.57 = f32[512,960]{0,1:T(8,128)} fusion(bf16[2560,960]{1,0:T(8,128)(2,1)} %bitcast.1, s32[2560]{0:T(1024)S(1)} %add.92, bf16[512,2560]{1,0:T(8,128)(2,1)} %param.10, f32[2560]{0:T(1024)S(1)} %copy-done.7, f32[512]{0:T(512)S(1)} %add_rsqrt_fusion), kind=kOutput, calls=%fused_computation.79 | convolution fusion | flops 9240576000 | bytes 9525248 | tf_op jit(solution)/shard_map/dot_general | solution.py:79
  110.9 1.9 select_bitcast_fusion
  112.8 0.7 multiply_subtract_fusion
  113.5 1.0 subtract_convert_fusion
  114.5 7.8 %fusion.52 = (f32[2,4,512]{2,1,0:T(4,128)S(1)}, f32[2,4,512,512]{2,3,1,0:T(8,128)}) fusion(pred[512,512]{0,1:T(8,128)(4,1)} %fusion.27, bf16[512,2,4,40]{0,3,2,1:T(8,128)(2,1)} %bitcast.68, bf16[512,2,4,40]{0,3,2,1:T(8,128)(2,1)} %bitcast.67, bf16[512,2,40]{0,2,1:T(8,128)(2,1)} %get-tuple-element.13, bf16[512,2,40]{0,2,1:T(8,128)(2,1)S(1)} %get-tuple-element.12), kind=kOutput, calls=%fused_computation.78 | convolution fusion | flops 345571840 | bytes 9486336 | tf_op jit(solution)/shard_map/sub | solution.py:96
  122.3 4.2 %fusion.23 = bf16[2,80,4,512]{3,1,2,0:T(8,128)(2,1)S(1)} fusion(bf16[512,2,80,1]{0,2,3,1:T(8,128)(2,1)S(1)} %bitcast.69, f32[2,4,512,512]{2,3,1,0:T(8,128)} %get-tuple-element.17, f32[2,4,512]{2,1,0:T(4,128)S(1)} %get-tuple-element.16), kind=kOutput, calls=%fused_computation.30 | convolution fusion | flops 340066304 | bytes 9224192 | tf_op jit(solution)/shard_map/kgqs,skd->qkgd/dot_general | solution.py:97
  126.5 3.8 convolution_convert_fusion.1
  130.4 32.8 %reduce-scatter.3.cloned.1.call-done = bf16[128,2560]{1,0:T(8,128)(2,1)} async-done(((bf16[512,2560]{1,0:T(8,128)(2,1)}), bf16[128,2560]{1,0:T(8,128)(2,1)}) %reduce-scatter.3.cloned.1.call-update) | async-done | bytes 655376 | tf_op jit(solution)/shard_map/reduce_scatter | solution.py:105
  163.2 1.6 multiply_reduce_fusion
  164.8 8.0 %fusion.17 = bf16[128,2560]{1,0:T(8,128)(2,1)} fusion(s32[2560]{0:T(1024)S(1)} %add.92, bf16[128,2560]{1,0:T(8,128)(2,1)} %reduce-scatter.3.cloned.1.call-done, f32[2560]{0:T(1024)S(1)} %copy-done.8, f32[128]{0:T(128)S(1)} %add_rsqrt_fusion.1, bf16[512,2560]{1,0:T(8,128)(2,1)} %param.10, s32[]{:T(128)S(6)} %select_n.15), kind=kOutput, calls=%fused_computation.26 | convolution fusion | flops 1686568960 | bytes 1987076 | tf_op jit(solution)/shard_map/dot_general | solution.py:111
  173.3 12.4 %all_to_all.41 = bf16[20,4,3456]{2,0,1:T(8,128)(2,1)S(1)} all-to-all(bf16[20,4,3456]{2,0,1:T(8,128)(2,1)S(1)} %copy.20), channel_id=1, replica_groups=mesh['req'=32,'tp'=4] {'tp'}, dimensions={1} | all-to-all | bytes 1105920 | tf_op jit(solution)/shard_map/all_to_all | solution.py:66
  185.7 0.9 all_to_all.36
  186.9 0.7 pad_maximum_fusion.7
  187.9 20.5 %all-gather.4.cloned.1.call-done = bf16[512,2560]{1,0:T(8,128)(2,1)} async-done(((bf16[128,2560]{1,0:T(8,128)(2,1)}), bf16[512,2560]{1,0:T(8,128)(2,1)}) %all-gather.4.cloned.1.call-update) | async-done | bytes 2621456 | tf_op jit(solution)/shard_map/all_gather | solution.py:112
  208.4 77.1 %all-gather.6.cloned.1.call-done = bf16[2560,3456]{1,0:T(8,128)(2,1)} async-done(((bf16[80,3456]{1,0:T(8,128)(2,1)}), bf16[2560,3456]{1,0:T(8,128)(2,1)}) %all-gather.6.cloned.1.call-update) | async-done | bytes 17694736 | tf_op jit(solution)/shard_map/all_gather | solution.py:78
  285.4 14.5 %fusion.58 = f32[512,3456]{1,0:T(8,128)S(1)} fusion(bf16[512,2560]{1,0:T(8,128)(2,1)} %all-gather.4.cloned.1.call-done, bf16[2560,3456]{1,0:T(8,128)(2,1)} %all-gather.6.cloned.1.call-done), kind=kOutput, calls=%fused_computation.80 | convolution fusion | flops 9059696640 | bytes 27394048 | tf_op jit(solution)/shard_map/dot_general | solution.py:113
  300.0 10.0 %convolution_convert_fusion = bf16[512,2560]{1,0:T(8,128)(2,1)} fusion(bf16[1728,2560]{1,0:T(8,128)(2,1)} %param.19, f32[512,3456]{1,0:T(8,128)S(1)} %fusion.58), kind=kOutput, calls=%fused_computation.18 | convolution fusion | flops 4536467456 | bytes 18808832 | tf_op jit(solution)/shard_map/dot_general | solution.py:115
  310.0 35.4 %all-gather.8.cloned.1.call-done = bf16[128,128,320]{1,2,0:T(8,128)(2,1)} async-done(((bf16[4,128,320]{1,2,0:T(8,128)(2,1)}), bf16[128,128,320]{1,2,0:T(8,128)(2,1)}) %all-gather.8.cloned.1.call-update) | async-done | bytes 10485776 | tf_op jit(solution)/shard_map/all_gather | solution.py:140
  345.5 9.8 %fusion.24 = bf16[4,128,320]{1,0,2:T(4,128)(2,1)S(1)} fusion(bf16[128,128,320]{1,2,0:T(8,128)(2,1)} %all-gather.8.cloned.1.call-done, s32[128]{0:T(128)S(1)} %copy-done.6, s32[4]{0:T(128)S(1)} %iota_add_fusion.1), kind=kOutput, calls=%fused_computation.35 | convolution fusion | flops 42107392 | bytes 10813968 | tf_op jit(solution)/shard_map/np,nsc->psc/dot_general | solution.py:137
  355.2 0.8 copy.24
  356.0 24.9 %reduce-scatter.5.cloned.1.call-done = bf16[128,2560]{1,0:T(8,128)(2,1)} async-done(((bf16[512,2560]{1,0:T(8,128)(2,1)}), bf16[128,2560]{1,0:T(8,128)(2,1)}) %reduce-scatter.5.cloned.1.call-update) | async-done | bytes 655376 | tf_op jit(solution)/shard_map/reduce_scatter | solution.py:116
  380.9 2.6 multiply_convert_fusion
  (52 shorter events, 1.7 us)
Async XLA Ops:
  7.2 119.4 %copy-start = (bf16[640,2560]{1,0:T(8,128)(2,1)S(1)}, bf16[640,2560]{1,0:T(8,128)(2,1)}, u32[]{:S(2)}) copy-start(bf16[640,2560]{1,0:T(8,128)(2,1)} %param.18) | copy-start | bytes 9830404
  24.9 10.3 %copy-start.9 = (s32[128]{0:T(128)S(1)}, s32[128]{0:T(128)}, u32[]{:S(2)}) copy-start(s32[128]{0:T(128)} %param.13) | copy-start | bytes 1540
  24.9 71.7 %copy-start.7 = (f32[2560]{0:T(1024)S(1)}, f32[2560]{0:T(1024)}, u32[]{:S(2)}) copy-start(f32[2560]{0:T(1024)} %param.16) | copy-start | bytes 30724
  24.9 71.7 %all-to-all-start.1 = ((bf16[32,80,960]{2,1,0:T(8,128)(2,1)}), bf16[32,80,960]{2,1,0:T(8,128)(2,1)}, u32[]{:S(2)}, u32[]{:S(2)}) async-start(bf16[32,80,960]{2,1,0:T(8,128)(2,1)} %stack.5), calls=%async_computation.1 | async-start | bytes 10485760 | tf_op jit(solution)/shard_map/all_to_all | solution.py:14
  35.1 128.1 %reduce-scatter.3.cloned.1.call-start = ((), (), s32[]{:S(2)}) async-start(), calls=%async_computation.5 | async-start | bytes 3276800 | tf_op jit(solution)/shard_map/reduce_scatter | solution.py:105
  110.9 1.9 slice-start
  110.9 2.5 slice-start.1
  114.5 7.8 %copy-start.5 = (bf16[512,160]{0,1:T(8,128)(2,1)S(1)}, bf16[512,160]{0,1:T(8,128)(2,1)}, u32[]{:S(2)}) copy-start(bf16[512,160]{0,1:T(8,128)(2,1)} %get-tuple-element.9) | copy-start | bytes 491524
  126.5 38.2 %copy-start.8 = (f32[2560]{0:T(1024)S(1)}, f32[2560]{0:T(1024)}, u32[]{:S(2)}) copy-start(f32[2560]{0:T(1024)} %param.17) | copy-start | bytes 30724
  130.3 78.1 %all-gather.4.cloned.1.call-start = ((), (), s32[]{:S(2)}) async-start(), calls=%async_computation.6 | async-start | bytes 3276800 | tf_op jit(solution)/shard_map/all_gather | solution.py:112
  164.8 8.1 %copy-start.2 = (f32[20,13824]{1,0:T(8,128)S(1)}, f32[20,13824]{1,0:T(8,128)}, u32[]{:S(2)}) copy-start(f32[20,13824]{1,0:T(8,128)} %param.15) | copy-start | bytes 3317764
  172.8 13.9 %copy-start.4 = (bf16[512,2,40]{0,2,1:T(8,128)(2,1)S(1)}, bf16[512,2,40]{0,2,1:T(8,128)(2,1)}, u32[]{:S(2)}) copy-start(bf16[512,2,40]{0,2,1:T(8,128)(2,1)} %get-tuple-element.13) | copy-start | bytes 245764
  172.8 14.0 %copy-start.3 = (bf16[20,4,8,128]{3,2,1,0:T(8,128)(2,1)S(1)}, bf16[20,4,8,128]{3,2,1,0:T(8,128)(2,1)}, u32[]{:S(2)}) copy-start(bf16[20,4,8,128]{3,2,1,0:T(8,128)(2,1)} %get-tuple-element.8) | copy-start | bytes 491524
  172.8 112.6 %all-gather.6.cloned.1.call-start = ((), (), s32[]{:S(2)}) async-start(), calls=%async_computation.7 | async-start | bytes 18247680 | tf_op jit(solution)/shard_map/all_gather | solution.py:78
  186.6 158.8 %all-gather.8.cloned.1.call-start = ((), (), s32[]{:S(2)}) async-start(), calls=%async_computation.9 | async-start | bytes 10813440 | tf_op jit(solution)/shard_map/all_gather | solution.py:140
  187.6 193.3 %reduce-scatter.5.cloned.1.call-start = ((), (), s32[]{:S(2)}) async-start(), calls=%async_computation.8 | async-start | bytes 3276800 | tf_op jit(solution)/shard_map/reduce_scatter | solution.py:116
  300.0 45.5 %copy-start.6 = (s32[128]{0:T(128)S(1)}, s32[128]{0:T(128)}, u32[]{:S(2)}) copy-start(s32[128]{0:T(128)} %param.12) | copy-start | bytes 1540
  345.5 38.0 %copy-start.1 = (bf16[640,2560]{1,0:T(8,128)(2,1)S(1)}, bf16[640,2560]{1,0:T(8,128)(2,1)}, u32[]{:S(2)}) copy-start(bf16[640,2560]{1,0:T(8,128)(2,1)} %param.18) | copy-start | bytes 9830404
Sparse Core Ops, SparseCore 0:
  130.4 32.6 reduce-scatter.2
  172.9 35.4 all-gather.3
  210.7 74.6 all-gather.5
  288.1 57.3 all-gather.7
  347.7 33.1 reduce-scatter.4
